TPU v7x, 32 devices: a whole 2x2x4 slice. The times are simulated.
32 devices in a mesh: rows: 8 (over z, y), cols: 4 (over x, core).
Axes of the slice: x: 2, y: 2, z: 4, core: 2. Of those that a mesh axis runs over, the one named last changes fastest.
Arguments:
- snapshot: float32 [3072, 8192], P('rows', 'cols'), may hold values from -270 to 270
- test_matrix: float32 [8192, 256], P('cols'), may hold values from -0.0625 to 0.0625
Outputs:
- projected: float32 [8192, 256], P('cols')
- triangle: float32 [256, 256], replicated
All inputs are finite; a program needn't handle non-finite values.
Results may differ from a plain program's by a relative error of at most 0.00007.
Values sent between devices are 32-bit elements; how exact they have to be, the bound alone decides.
No kernel may reach another device: no remote copies, remote signals or barrier semaphores. Data moves between devices by JAX's collectives and lax.ppermute only.
A program may use at most 64 MiB of HBM per device.

v0:
```python
import jax
import jax.numpy as jnp
from jax import lax
from jax.sharding import PartitionSpec as P

high = lax.Precision.HIGHEST


def inner(left, right):
    return jnp.dot(left.T, right, precision=high, preferred_element_type=jnp.float32)


def body(snapshot, test_matrix):
    partial_sketch = jnp.dot(
        snapshot, test_matrix, precision=high, preferred_element_type=jnp.float32
    )
    sketch = lax.psum(partial_sketch, "cols")
    local_gram = inner(sketch, sketch)
    gram = lax.psum(local_gram, "rows")
    lower = jnp.linalg.cholesky(gram)
    basis = jax.scipy.linalg.solve_triangular(lower, sketch.T, lower=True).T
    projected = lax.psum(inner(snapshot, basis), "rows")
    total = snapshot.shape[0] * lax.axis_size("rows")
    triangle = lower.T / jnp.sqrt(jnp.float32(total))
    return (projected, triangle)


def solution(mesh):
    return jax.shard_map(
        body,
        mesh=mesh,
        in_specs=(P("rows", "cols"), P("cols", None)),
        out_specs=(P("cols", None), P()),
        check_vma=False,
    )
```

profile of v0, /device:TPU:0, one launch (start us, length us, event | category | flops | bytes accessed | tf_op | source)
XLA Modules:
  0.0 326.2 jit_solution(9881222707864030921)
XLA Ops:
  7.2 1.8 copy-done
  9.1 5.0 %fusion.14 = f32[384,256]{1,0:T(8,128)} fusion(f32[384,2048]{1,0:T(8,128)S(1)} %copy-done, f32[2048,256]{1,0:T(8,128)} %param.3), kind=kOutput, calls=%fused_computation.35 | convolution fusion | flops 2415919104 | bytes 5636096 | tf_op jit(solution)/shard_map/dot_general | solution.py:14
  14.1 35.6 %all-reduce.5.cloned.1.call-done = f32[384,256]{1,0:T(8,128)} async-done(((f32[384,256]{1,0:T(8,128)}), f32[384,256]{1,0:T(8,128)}) %all-reduce.5.cloned.1.call-update) | async-done | bytes 393232 | tf_op jit(solution)/shard_map/psum | solution.py:17
  49.8 2.7 fusion.15
  52.7 72.0 %all-reduce.7.cloned.1.call-done = f32[256,256]{0,1:T(8,128)} async-done(((f32[256,256]{0,1:T(8,128)}), f32[256,256]{0,1:T(8,128)}) %all-reduce.7.cloned.1.call-update) | async-done | bytes 262160 | tf_op jit(solution)/shard_map/psum | solution.py:19
  124.7 1.8 copy.5
  126.5 1.1 fusion.3
  127.6 0.7 copy-done.3
  128.9 13.2 %cholesky.50 = f32[128,128]{1,0:T(8,128)} custom-call(f32[128,128]{1,0:T(8,128)} %cholesky.118), custom_call_target="Cholesky" | custom-call | tf_op jit(solution)/shard_map/jit(cholesky)/cholesky | solution.py:20
  142.1 1.5 select_reduce_fusion.1
  143.6 11.3 %custom-call.15 = f32[1,128,128]{1,2,0:T(8,128)} custom-call(f32[1,128,128]{2,1,0:T(8,128)} %get-tuple-element.27), custom_call_target="InvertDiagBlocksLowerTriangular" | custom-call | tf_op jit(solution)/shard_map/jit(cholesky)/cholesky | solution.py:20
  154.9 1.6 cholesky.113
  156.4 1.7 constant_dynamic-update-slice_fusion.1
  158.1 1.7 convolution_subtract_fusion.1
  159.8 13.2 %cholesky.105 = f32[128,128]{1,0:T(8,128)} custom-call(f32[128,128]{1,0:T(8,128)} %convolution_subtract_fusion.1), custom_call_target="Cholesky" | custom-call | tf_op jit(solution)/shard_map/jit(cholesky)/cholesky | solution.py:20
  173.0 1.5 select_reduce_fusion
  174.5 0.7 compare_reduce_fusion
  176.5 1.8 multiply_bitcast_fusion
  178.3 7.0 %while.1 = (s32[]{:T(128)}, f32[256,256]{1,0:T(8,128)}, s32[2,2]{1,0:T(2,128)S(1)}, f32[2,128,128]{2,1,0:T(8,128)}, s32[]{:T(128)}) while((s32[]{:T(128)}, f32[256,256]{1,0:T(8,128)}, s32[2,2]{1,0:T(2,128)S(1)}, f32[2,128,128]{2,1,0:T(8,128)}, s32[]{:T(128)}) %tuple.29), condition=%wide.while_cond, body=%wide.while_body.sunk | while | flops 2 | bytes 132205 | solution.py:21
  178.4 0.6 fusion.26
  179.0 2.9 bitcast_dynamic-update-slice_fusion.2
  181.9 0.6 fusion.26
  182.5 2.8 bitcast_dynamic-update-slice_fusion.2
  185.3 21.1 %custom-call.16 = f32[2,128,128]{1,2,0:T(8,128)} custom-call(f32[2,128,128]{2,1,0:T(8,128)} %get-tuple-element.9), custom_call_target="InvertDiagBlocksLowerTriangular" | custom-call | tf_op jit(solution)/shard_map/jit(_solve_triangular)/triangular_solve | solution.py:21
  206.4 1.2 fusion.5
  207.7 1.3 convolution_subtract_fusion
  209.0 1.2 fusion.8
  210.2 4.9 %convolution_bitcast_fusion = f32[2048,256]{0,1:T(8,128)} fusion(f32[384,2048]{1,0:T(8,128)S(1)} %copy-done, f32[128,384]{1,0:T(8,128)S(1)} %fusion.8, f32[128,384]{1,0:T(8,128)S(1)} %fusion.5), kind=kOutput, calls=%fused_computation.2 | convolution fusion | flops 2416017408 | bytes 5636096 | tf_op jit(solution)/shard_map/dot_general | solution.py:10
  215.1 0.9 copy-done.2
  216.1 0.8 copy.7
  216.9 99.9 %all-reduce.9.cloned.1.call-done = f32[2048,256]{0,1:T(8,128)} async-done(((f32[2048,256]{0,1:T(8,128)}), f32[2048,256]{0,1:T(8,128)}) %all-reduce.9.cloned.1.call-update) | async-done | bytes 2097168 | tf_op jit(solution)/shard_map/psum | solution.py:22
  316.8 2.9 copy.6
  (17 shorter events, 1.1 us)
Async XLA Ops:
  7.2 1.9 copy-start
  7.2 42.6 %all-reduce.5.cloned.1.call-start = ((), (), s32[]{:S(2)}) async-start(), calls=%async_computation | async-start | bytes 786432 | tf_op jit(solution)/shard_map/psum | solution.py:17
  14.1 110.7 %all-reduce.7.cloned.1.call-start = ((), (), s32[]{:S(2)}) async-start(), calls=%async_computation.1 | async-start | bytes 524288 | tf_op jit(solution)/shard_map/psum | solution.py:19
  52.5 264.3 %all-reduce.9.cloned.1.call-start = ((), (), s32[]{:S(2)}) async-start(), calls=%async_computation.2 | async-start | bytes 4194304 | tf_op jit(solution)/shard_map/psum | solution.py:22
  52.7 153.7 %copy-start.1 = (f32[384,256]{1,0:T(8,128)S(1)}, f32[384,256]{1,0:T(8,128)}, u32[]{:S(2)}) copy-start(f32[384,256]{1,0:T(8,128)} %all-reduce.5.cloned.1.call-done) | copy-start | bytes 1179652
  127.6 0.7 copy-start.3
  215.1 0.9 copy-start.2
Sparse Core Ops, SparseCore 0:
  14.2 35.5 all-reduce.4
  53.7 71.0 all-reduce.6
  215.3 101.4 all-reduce.8
where the time goes:
time: 327 us; the launch traced here: 326 us
  waiting for transfers between devices  208 us (64%)
  other arithmetic  65.2 us (20%)
  matrix products  19.8 us (6%)
  local copies, waits for them, and re-layouts  18.2 us (6%)
  between operations  15.1 us (5%)
    psum x1, waiting for transfers between devices, body(): projected = lax.psum(inner(snapshot, basis), 'rows')  99.9 us
    psum x1, waiting for transfers between devices, body(): gram = lax.psum(local_gram, 'rows')  72 us
    another operation x6, other arithmetic, body(): lower = jnp.linalg.cholesky(gram)  41.3 us
    psum x1, waiting for transfers between devices, body(): sketch = lax.psum(partial_sketch, 'cols')  35.6 us
    another operation x2, other arithmetic, body(): basis = jax.scipy.linalg.solve_triangular(lower, sketch.T, lower=True).T  21.1 us
    dot_general x2, matrix products, inner(): jnp.dot(left.T, right, precision=high, preferred_element_type=jnp.float32)  7.53 us
    unnamed x10, local copies, waits for them, and re-layouts  7.18 us
    another operation x6, local copies, waits for them, and re-layouts  6.98 us
  transfers between devices with their start and end apart: 3, of which 3 were waited for; matrix products, arithmetic and copies ran while one was open for 0% of the time, Pallas kernels for 0%

commit v1 on v0

--- a/solution.py
+++ b/solution.py
@@ -16,7 +16,7 @@
     )
     sketch = lax.psum(partial_sketch, "cols")
     local_gram = inner(sketch, sketch)
-    gram = lax.psum(local_gram, "rows")
+    gram = jnp.sum(lax.all_gather(local_gram, "rows"), axis=0)
     lower = jnp.linalg.cholesky(gram)
     basis = jax.scipy.linalg.solve_triangular(lower, sketch.T, lower=True).T
     projected = lax.psum(inner(snapshot, basis), "rows")

time: 327 us -> 306 us (0.936)
  waiting for transfers between devices: 208 us -> 184 us
    psum x1 -> x0, waiting for transfers between devices: 72 us -> none  [body(): gram = lax.psum(local_gram, 'rows')]
    all_gather x0 -> x1, waiting for transfers between devices: none -> 49 us  [body(): gram = jnp.sum(lax.all_gather(local_gram, 'rows'), axis=0)]
where the time goes in v1:
time: 306 us; the launch traced here: 305 us
  waiting for transfers between devices  184 us (60%)
  other arithmetic  67.7 us (22%)
  matrix products  19.7 us (6%)
  local copies, waits for them, and re-layouts  18.3 us (6%)
  between operations  15.2 us (5%)
    psum x1, waiting for transfers between devices, body(): projected = lax.psum(inner(snapshot, basis), 'rows')  99.2 us
    all_gather x1, waiting for transfers between devices, body(): gram = jnp.sum(lax.all_gather(local_gram, 'rows'), axis=0)  49 us
    another operation x6, other arithmetic, body(): lower = jnp.linalg.cholesky(gram)  41.3 us
    psum x1, waiting for transfers between devices, body(): sketch = lax.psum(partial_sketch, 'cols')  35.6 us
    another operation x2, other arithmetic, body(): basis = jax.scipy.linalg.solve_triangular(lower, sketch.T, lower=True).T  21.1 us
    dot_general x2, matrix products, inner(): jnp.dot(left.T, right, precision=high, preferred_element_type=jnp.float32)  7.51 us
    unnamed x10, local copies, waits for them, and re-layouts  7.18 us
    another operation x6, local copies, waits for them, and re-layouts  7.01 us
  transfers between devices with their start and end apart: 3, of which 3 were waited for; matrix products, arithmetic and copies ran while one was open for 0% of the time, Pallas kernels for 0%

profile of v1, /device:TPU:0, one launch (start us, length us, event | category | flops | bytes accessed | tf_op | source)
XLA Modules:
  0.0 305.1 jit_solution(765360380445050285)
XLA Ops:
  7.2 1.8 copy-done
  9.1 5.0 %fusion.14 = f32[384,256]{1,0:T(8,128)} fusion(f32[384,2048]{1,0:T(8,128)S(1)} %copy-done, f32[2048,256]{1,0:T(8,128)} %param.3), kind=kOutput, calls=%fused_computation.35 | convolution fusion | flops 2415919104 | bytes 5636096 | tf_op jit(solution)/shard_map/dot_general | solution.py:14
  14.1 35.6 %all-reduce.4.cloned.1.call-done = f32[384,256]{1,0:T(8,128)} async-done(((f32[384,256]{1,0:T(8,128)}), f32[384,256]{1,0:T(8,128)}) %all-reduce.4.cloned.1.call-update) | async-done | bytes 393232 | tf_op jit(solution)/shard_map/psum | solution.py:17
  49.8 2.6 fusion.15
  52.7 49.0 %all-gather.3.cloned.1.call-done = f32[2048,256]{1,0:T(8,128)} async-done(((f32[256,256]{1,0:T(8,128)}), f32[2048,256]{1,0:T(8,128)}) %all-gather.3.cloned.1.call-update) | async-done | bytes 2097168 | tf_op jit(solution)/shard_map/all_gather | solution.py:19
  101.7 2.5 reduce_sum.9
  104.1 1.8 copy.7
  106.0 1.1 fusion.3
  107.1 0.7 copy-done.3
  108.4 13.2 %cholesky.50 = f32[128,128]{1,0:T(8,128)} custom-call(f32[128,128]{1,0:T(8,128)} %cholesky.118), custom_call_target="Cholesky" | custom-call | tf_op jit(solution)/shard_map/jit(cholesky)/cholesky | solution.py:20
  121.6 1.5 select_reduce_fusion.1
  123.0 1.6 cholesky.113
  124.6 11.3 %custom-call.15 = f32[1,128,128]{1,2,0:T(8,128)} custom-call(f32[1,128,128]{2,1,0:T(8,128)} %get-tuple-element.29), custom_call_target="InvertDiagBlocksLowerTriangular" | custom-call | tf_op jit(solution)/shard_map/jit(cholesky)/cholesky | solution.py:20
  135.9 1.7 constant_dynamic-update-slice_fusion.1
  137.6 1.7 convolution_subtract_fusion.1
  139.3 13.2 %cholesky.105 = f32[128,128]{1,0:T(8,128)} custom-call(f32[128,128]{1,0:T(8,128)} %convolution_subtract_fusion.1), custom_call_target="Cholesky" | custom-call | tf_op jit(solution)/shard_map/jit(cholesky)/cholesky | solution.py:20
  152.5 1.5 select_reduce_fusion
  154.0 0.7 compare_reduce_fusion
  156.0 1.8 multiply_bitcast_fusion
  157.9 7.0 %while.1 = (s32[]{:T(128)}, f32[256,256]{1,0:T(8,128)}, s32[2,2]{1,0:T(2,128)S(1)}, f32[2,128,128]{2,1,0:T(8,128)}, s32[]{:T(128)}) while((s32[]{:T(128)}, f32[256,256]{1,0:T(8,128)}, s32[2,2]{1,0:T(2,128)S(1)}, f32[2,128,128]{2,1,0:T(8,128)}, s32[]{:T(128)}) %tuple.30), condition=%wide.while_cond, body=%wide.while_body.sunk | while | flops 2 | bytes 132205 | solution.py:21
  157.9 0.7 fusion.26
  158.6 2.9 bitcast_dynamic-update-slice_fusion.2
  162.1 2.8 bitcast_dynamic-update-slice_fusion.2
  164.9 21.1 %custom-call.16 = f32[2,128,128]{1,2,0:T(8,128)} custom-call(f32[2,128,128]{2,1,0:T(8,128)} %get-tuple-element.9), custom_call_target="InvertDiagBlocksLowerTriangular" | custom-call | tf_op jit(solution)/shard_map/jit(_solve_triangular)/triangular_solve | solution.py:21
  186.0 1.2 fusion.5
  187.2 1.3 convolution_subtract_fusion
  188.6 1.2 fusion.8
  189.8 4.9 %convolution_bitcast_fusion = f32[2048,256]{0,1:T(8,128)} fusion(f32[384,2048]{1,0:T(8,128)S(1)} %copy-done, f32[128,384]{1,0:T(8,128)S(1)} %fusion.8, f32[128,384]{1,0:T(8,128)S(1)} %fusion.5), kind=kOutput, calls=%fused_computation.2 | convolution fusion | flops 2416017408 | bytes 5636096 | tf_op jit(solution)/shard_map/dot_general | solution.py:10
  194.7 0.9 copy-done.2
  195.6 0.8 copy.9
  196.5 99.2 %all-reduce.6.cloned.1.call-done = f32[2048,256]{0,1:T(8,128)} async-done(((f32[2048,256]{0,1:T(8,128)}), f32[2048,256]{0,1:T(8,128)}) %all-reduce.6.cloned.1.call-update) | async-done | bytes 2097168 | tf_op jit(solution)/shard_map/psum | solution.py:22
  295.7 2.9 copy.8
  (18 shorter events, 1.8 us)
Async XLA Ops:
  7.2 1.9 copy-start
  7.2 42.6 %all-reduce.4.cloned.1.call-start = ((), (), s32[]{:S(2)}) async-start(), calls=%async_computation | async-start | bytes 786432 | tf_op jit(solution)/shard_map/psum | solution.py:17
  14.1 87.6 %all-gather.3.cloned.1.call-start = ((), (), s32[]{:S(2)}) async-start(), calls=%async_computation.2 | async-start | bytes 2359296 | tf_op jit(solution)/shard_map/all_gather | solution.py:19
  52.4 243.2 %all-reduce.6.cloned.1.call-start = ((), (), s32[]{:S(2)}) async-start(), calls=%async_computation.1 | async-start | bytes 4194304 | tf_op jit(solution)/shard_map/psum | solution.py:22
  104.1 81.8 %copy-start.1 = (f32[384,256]{1,0:T(8,128)S(1)}, f32[384,256]{1,0:T(8,128)}, u32[]{:S(2)}) copy-start(f32[384,256]{1,0:T(8,128)} %all-reduce.4.cloned.1.call-done) | copy-start | bytes 1179652
  107.1 0.7 copy-start.3
  194.7 0.9 copy-start.2
Sparse Core Ops, SparseCore 0:
  14.2 35.5 all-reduce.3
  52.6 49.0 all-gather.2
  194.8 100.7 all-reduce.5
